TPU v7x, 512 devices: a whole 4x8x8 slice. The times are simulated.
512 devices in a mesh: dp: 32 (over x, y), table: 16 (over z, core).
Axes of the slice: x: 4, y: 8, z: 8, core: 2. Of those that a mesh axis runs over, the one named last changes fastest.
Arguments:
- table: bfloat16 [12288, 512], P('table'), may hold values from -6 to 6
- history_shard: int32 [512, 256, 1], P(('dp', 'table')), may hold values from 0 to 15; in each aligned block of 256 rows (0 to 255, 256 to 511, ..., all dimensions but the last counted through in order) at most 32 rows name the same one
- history_row: int32 [512, 256], P(('dp', 'table')), may hold values from 0 to 767
- lengths: int32 [512], P(('dp', 'table')), may hold values from 1 to 256, 98304 in all
- w_in: bfloat16 [512, 2048], replicated, may hold values from -0.25 to 0.25
- w_out: bfloat16 [512, 512], replicated, may hold values from -0.25 to 0.25
- cotangent: bfloat16 [512, 256, 512], P(('dp', 'table')), may hold values from -6 to 6
Outputs:
- table_grad: float32 [12288, 512], P('table')
- dense_grad: bfloat16 [512, 512], replicated
Inputs may be any that keep to these rules, and one draw needn't show every extreme that they name: `history_shard`: among the 256 history slots of one device's samples, at most 32 name one table shard, and that bound is met by some shard in some device's slots. `lengths`: some sample has the full length 256.
All inputs are finite; a program needn't handle non-finite values. No bound on the sum of `lengths` on one device may be relied on, other than what follows from the above.
Results may differ from a plain program's by a relative error of at most 0.017.
Values may be sent and summed in bfloat16 or wider, within the bound.
A program may use at most 64 MiB of HBM per device.

v0:
```python
import math
import jax
import jax.numpy as jnp
from jax import lax
from jax.sharding import PartitionSpec as P

HEADS = 4


def layer_norm(values):
    average = jnp.mean(values, axis=-1, keepdims=True)
    centred = values - average
    variance = jnp.mean(centred * centred, axis=-1, keepdims=True)
    return centred * lax.rsqrt(variance + 1e-06)


def hstu_layer(embedded, w_in, w_out, lengths):
    samples_here, seq_span, model_width = embedded.shape
    head_dim = model_width // HEADS
    normed = layer_norm(embedded.astype(jnp.float32)).astype(jnp.bfloat16)
    projected = jax.nn.silu(
        jnp.dot(
            normed.reshape(samples_here * seq_span, model_width),
            w_in,
            preferred_element_type=jnp.float32,
        )
    )
    gate_part = projected[:, :model_width]
    shaped = (samples_here, seq_span, HEADS, head_dim)
    values = projected[:, model_width : 2 * model_width].astype(jnp.bfloat16).reshape(shaped)
    queries = projected[:, 2 * model_width : 3 * model_width].astype(jnp.bfloat16).reshape(shaped)
    keys = projected[:, 3 * model_width :].astype(jnp.bfloat16).reshape(shaped)
    scores = jnp.einsum(
        "blhd,bmhd->bhlm", queries.astype(jnp.float32), keys.astype(jnp.float32)
    ) * head_dim ** (-0.5)
    positions = jnp.arange(seq_span)
    live_keys = (positions[None, None, :] <= positions[None, :, None]) & (
        positions[None, None, :] < lengths[:, None, None]
    )
    weights = (
        jnp.where(live_keys[:, None], jax.nn.silu(scores), 0.0)
        / lengths.astype(jnp.float32)[:, None, None, None]
    )
    weights = weights.astype(jnp.bfloat16)
    attended = jnp.einsum(
        "bhlm,bmhd->blhd", weights.astype(jnp.float32), values.astype(jnp.float32)
    ).reshape(samples_here * seq_span, model_width)
    mixed = (layer_norm(attended) * gate_part).astype(jnp.bfloat16)
    output = jnp.dot(mixed, w_out, preferred_element_type=jnp.float32) + embedded.reshape(
        -1, model_width
    ).astype(jnp.float32)
    return (output, mixed)


def pick_rows(index, length):
    return (index[:, None] == jnp.arange(length, dtype=jnp.int32)[None, :]).astype(jnp.bfloat16)


def per_device(table, history_shard, history_row, lengths, w_in, w_out, cotangent):
    shard_rows, model_width = table.shape
    samples_here, seq_span = history_row.shape
    groups = lax.axis_size("table")
    copies = lax.axis_size("dp")
    slot_count = samples_here * seq_span
    capacity = 2 * slot_count // groups
    owners = history_shard[:, :, 0].reshape(-1)
    local_rows = history_row.reshape(-1)
    owner_hits = (owners[:, None] == jnp.arange(groups)[None, :]).astype(jnp.int32)
    slot_rank = jnp.sum((jnp.cumsum(owner_hits, axis=0) - owner_hits) * owner_hits, axis=1)
    position = owners * capacity + slot_rank
    slot_hits = position[:, None] == jnp.arange(groups * capacity, dtype=jnp.int32)[None, :]
    requested = jnp.sum(jnp.where(slot_hits, local_rows[:, None], 0), axis=0).reshape(
        groups, capacity
    )
    incoming = lax.all_to_all(requested, "table", split_axis=0, concat_axis=0, tiled=True).reshape(
        -1
    )
    reply = jnp.dot(
        pick_rows(incoming, shard_rows), table, preferred_element_type=jnp.float32
    ).astype(jnp.bfloat16)
    received = lax.all_to_all(
        reply.reshape(groups, capacity, model_width),
        "table",
        split_axis=0,
        concat_axis=0,
        tiled=True,
    ).reshape(groups * capacity, model_width)
    place = slot_hits.astype(jnp.bfloat16)
    embedded = jnp.dot(place, received, preferred_element_type=jnp.float32).astype(jnp.bfloat16)
    embedded = embedded.reshape(samples_here, seq_span, model_width)
    output, pullback, mixed = jax.vjp(
        lambda rows_in: hstu_layer(rows_in, w_in, w_out, lengths), embedded, has_aux=True
    )
    row_live = jnp.arange(seq_span)[None, :] < lengths[:, None]
    grad_seed = jnp.where(row_live[:, :, None], cotangent, jnp.zeros_like(cotangent))
    flat_seed = grad_seed.reshape(-1, model_width)
    total_slots = slot_count * copies * groups
    grad_scale = 1.0 / math.sqrt(total_slots)
    dense_part = lax.dot_general(
        mixed, flat_seed, (((0,), (0,)), ((), ())), preferred_element_type=jnp.float32
    ).astype(jnp.bfloat16)
    dense_rows = model_width // groups
    dense_terms = lax.all_to_all(
        dense_part.reshape(groups, dense_rows, model_width),
        "table",
        split_axis=0,
        concat_axis=0,
        tiled=True,
    )
    dense_block = jnp.sum(dense_terms.astype(jnp.float32), axis=0).astype(jnp.bfloat16)
    dense_blocks = lax.all_gather(dense_block, "dp", axis=0, tiled=False)
    dense_sum = jnp.sum(dense_blocks.astype(jnp.float32), axis=0) * grad_scale
    dense_grad = lax.all_gather(dense_sum.astype(jnp.bfloat16), "table", axis=0, tiled=True)
    (row_grad,) = pullback(flat_seed.astype(jnp.float32))
    outgoing = lax.dot_general(
        place,
        row_grad.reshape(-1, model_width),
        (((0,), (0,)), ((), ())),
        preferred_element_type=jnp.float32,
    ).astype(jnp.bfloat16)
    arrived = lax.all_to_all(
        outgoing.reshape(groups, capacity, model_width),
        "table",
        split_axis=0,
        concat_axis=0,
        tiled=True,
    ).reshape(groups * capacity, model_width)
    local_grad = lax.dot_general(
        pick_rows(incoming, shard_rows),
        arrived,
        (((0,), (0,)), ((), ())),
        preferred_element_type=jnp.float32,
    ).astype(jnp.bfloat16)
    part_rows = shard_rows // copies
    terms = lax.all_to_all(
        local_grad.reshape(copies, part_rows, model_width),
        "dp",
        split_axis=0,
        concat_axis=0,
        tiled=True,
    )
    summed = jnp.sum(terms.astype(jnp.float32), axis=0).astype(jnp.bfloat16)
    table_grad = lax.all_gather(summed, "dp", axis=0, tiled=True).astype(jnp.float32)
    return (table_grad, dense_grad)


def solution(mesh):
    in_specs = (
        P("table", None),
        P(("dp", "table"), None, None),
        P(("dp", "table"), None),
        P(("dp", "table")),
        P(),
        P(),
        P(("dp", "table"), None, None),
    )
    out_specs = (P("table", None), P())
    return jax.shard_map(
        per_device, mesh=mesh, in_specs=in_specs, out_specs=out_specs, check_vma=False
    )
```

profile of v0, /device:TPU:1, one launch (start us, length us, event | category | flops | bytes accessed | tf_op | source)
XLA Modules:
  0.0 225.5 jit_solution(14855246301839063184)
XLA Ops:
  11.2 18.6 %all_to_all.29 = s32[16,1,32]{2,1,0:T(1,128)S(1)} all-to-all(s32[16,1,32]{2,1,0:T(1,128)S(1)} %all_to_all.18), channel_id=1, replica_groups=mesh['dp'=32,'table'=16] {'table'}, dimensions={0} | all-to-all | bytes 4096 | tf_op jit(solution)/shard_map/all_to_all | solution.py:75
  31.1 2.5 %fusion.17 = bf16[512,512]{1,0:T(8,128)(2,1)} fusion(bf16[768,512]{1,0:T(8,128)(2,1)} %param.7, s32[512]{0:T(512)S(1)} %eq.68), kind=kOutput, calls=%fused_computation.23 | convolution fusion | flops 403308544 | bytes 1312768 | tf_op jit(solution)/shard_map/dot_general | solution.py:78
  33.6 4.0 %all-to-all-start.1 = ((bf16[16,32,512]{2,1,0:T(8,128)(2,1)}), bf16[16,32,512]{2,1,0:T(8,128)(2,1)S(1)}, u32[]{:S(2)}, u32[]{:S(2)}) async-start(bf16[16,32,512]{2,1,0:T(8,128)(2,1)} %bitcast.6), calls=%async_computation.1 | async-start | bytes 1048576 | tf_op jit(solution)/shard_map/all_to_all | solution.py:81
  38.4 16.6 %all-to-all-done.1 = bf16[16,32,512]{2,1,0:T(8,128)(2,1)S(1)} async-done(((bf16[16,32,512]{2,1,0:T(8,128)(2,1)}), bf16[16,32,512]{2,1,0:T(8,128)(2,1)S(1)}, u32[]{:S(2)}, u32[]{:S(2)}) %all-to-all-start.1) | async-done | bytes 524320 | tf_op jit(solution)/shard_map/all_to_all | solution.py:81
  55.7 2.7 %fusion.70 = (bf16[256,2048]{1,0:T(8,128)(2,1)S(1)}, f32[256,2048]{1,0:T(8,128)}, f32[256,2048]{1,0:T(8,128)}) fusion(bf16[512,2048]{1,0:T(8,128)(2,1)S(1)} %copy-done, f32[256,512]{1,0:T(8,128)S(1)} %get-tuple-element.15, f32[256]{0:T(256)S(1)} %fusion.63, f32[256]{0:T(256)S(1)} %broadcast_multiply_fusion.1), kind=kOutput, calls=%fused_computation.113 | convolution fusion | flops 539885568 | bytes 7866368 | tf_op jit(solution)/shard_map/jvp()/dot_general | solution.py:22
  60.0 1.6 divide_convert_fusion
  62.7 1.2 copy.48
  64.0 1.8 multiply_reduce_fusion.1
  65.9 1.3 convolution_convert_fusion.1
  68.4 1.3 fusion.76
  69.7 2.0 fusion.31
  73.9 1.9 copy.50
  76.6 4.1 %all-to-all-start.4 = ((bf16[16,32,512]{2,1,0:T(8,128)(2,1)}), bf16[16,32,512]{2,1,0:T(8,128)(2,1)}, u32[]{:S(2)}, u32[]{:S(2)}) async-start(bf16[16,32,512]{2,1,0:T(8,128)(2,1)} %bitcast.30), calls=%async_computation.4 | async-start | bytes 1048576 | tf_op jit(solution)/shard_map/all_to_all | solution.py:103
  80.7 2.9 %multiply_reduce_fusion = (f32[256]{0:T(256)S(1)}, f32[256,512]{1,0:T(8,128)S(1)}) fusion(f32[256,512]{1,0:T(8,128)S(1)} %get-tuple-element.15, f32[256]{0:T(256)S(1)} %broadcast_multiply_fusion.1, bf16[512,2048]{1,0:T(8,128)(2,1)S(1)} %copy-done, f32[256,2048]{1,0:T(8,128)} %get-tuple-element.16, f32[256,512]{1,0:T(8,128)} %get-tuple-element.8, ...), kind=kOutput, calls=%fused_computation.56 | convolution fusion | flops 545390336 | bytes 6555648 | tf_op jit(solution)/shard_map/transpose(jvp())/dot_general | solution.py:22
  84.0 1.3 convolution_convert_fusion.2
  85.3 11.7 %all-to-all-done.4 = bf16[16,32,512]{2,1,0:T(8,128)(2,1)} async-done(((bf16[16,32,512]{2,1,0:T(8,128)(2,1)}), bf16[16,32,512]{2,1,0:T(8,128)(2,1)}, u32[]{:S(2)}, u32[]{:S(2)}) %all-to-all-start.4) | async-done | bytes 524320 | tf_op jit(solution)/shard_map/all_to_all | solution.py:103
  96.9 3.5 %all-to-all-start.2 = ((bf16[16,32,512]{2,1,0:T(8,128)(2,1)}), bf16[16,32,512]{2,1,0:T(8,128)(2,1)S(1)}, u32[]{:S(2)}, u32[]{:S(2)}) async-start(bf16[16,32,512]{2,1,0:T(8,128)(2,1)} %bitcast.27), calls=%async_computation.2 | async-start | bytes 1048576 | tf_op jit(solution)/shard_map/all_to_all | solution.py:121
  100.5 1.7 reduce_sum.150
  102.2 14.9 %all-to-all-done.2 = bf16[16,32,512]{2,1,0:T(8,128)(2,1)S(1)} async-done(((bf16[16,32,512]{2,1,0:T(8,128)(2,1)}), bf16[16,32,512]{2,1,0:T(8,128)(2,1)S(1)}, u32[]{:S(2)}, u32[]{:S(2)}) %all-to-all-start.2) | async-done | bytes 524320 | tf_op jit(solution)/shard_map/all_to_all | solution.py:121
  117.8 31.6 %all_to_all.30 = bf16[32,24,512]{2,1,0:T(8,128)(2,1)S(1)} all-to-all(bf16[32,24,512]{2,1,0:T(8,128)(2,1)S(1)} %bitcast.113), channel_id=1, replica_groups=mesh['dp'=32,'table'=16] {'dp'}, dimensions={0} | all-to-all | bytes 1572864 | tf_op jit(solution)/shard_map/all_to_all | solution.py:135
  149.5 40.4 %all_gather.12 = bf16[768,512]{1,0:T(8,128)(2,1)S(1)} all-gather(bf16[24,512]{1,0:T(8,128)(2,1)S(1)} %reduce_sum.149), channel_id=1, replica_groups=mesh['dp'=32,'table'=16] {'dp'}, dimensions={0}, use_global_device_ids=true | all-gather | bytes 811008 | tf_op jit(solution)/shard_map/all_gather | solution.py:143
  189.9 1.4 convert_element_type.164
  191.3 1.4 convert_reduce_fusion
  192.7 25.2 %all_gather.15 = bf16[512,512]{1,0:T(8,128)(2,1)S(1)} all-gather(bf16[32,512]{1,0:T(8,128)(2,1)S(1)} %multiply_convert_fusion.4), channel_id=1, replica_groups=mesh['dp'=32,'table'=16] {'table'}, dimensions={0}, use_global_device_ids=true | all-gather | bytes 557056 | tf_op jit(solution)/shard_map/all_gather | solution.py:113
  (65 shorter events, 15.0 us)
Async XLA Ops:
  7.2 48.5 %copy-start = (bf16[512,2048]{1,0:T(8,128)(2,1)S(1)}, bf16[512,2048]{1,0:T(8,128)(2,1)}, u32[]{:S(2)}) copy-start(bf16[512,2048]{1,0:T(8,128)(2,1)} %param.11) | copy-start | bytes 6291460
  33.6 21.4 %all-to-all-start.1 = ((bf16[16,32,512]{2,1,0:T(8,128)(2,1)}), bf16[16,32,512]{2,1,0:T(8,128)(2,1)S(1)}, u32[]{:S(2)}, u32[]{:S(2)}) async-start(bf16[16,32,512]{2,1,0:T(8,128)(2,1)} %bitcast.6), calls=%async_computation.1 | async-start | bytes 1048576 | tf_op jit(solution)/shard_map/all_to_all | solution.py:81
  59.3 0.7 copy-start.5
  59.4 2.1 copy-start.7
  60.0 1.6 copy-start.9
  61.6 0.8 copy-start.3
  61.6 2.4 %copy-start.2 = (bf16[1,256,512]{2,1,0:T(8,128)(2,1)S(1)}, bf16[1,256,512]{2,1,0:T(8,128)(2,1)}, u32[]{:S(2)}) copy-start(bf16[1,256,512]{2,1,0:T(8,128)(2,1)} %param.13) | copy-start | bytes 786436
  61.9 0.8 copy-start.1
  64.0 1.9 copy-start.4
  69.7 2.1 copy-start.6
  69.7 2.4 %copy-start.8 = (bf16[256,512]{0,1:T(8,128)(2,1)S(1)}, bf16[256,512]{0,1:T(8,128)(2,1)}, u32[]{:S(2)}) copy-start(bf16[256,512]{0,1:T(8,128)(2,1)} %copy-done.7) | copy-start | bytes 786436
  73.9 6.9 %copy-start.10 = (bf16[256,512]{1,0:T(8,128)(2,1)S(1)}, bf16[256,512]{1,0:T(8,128)(2,1)}, u32[]{:S(2)}) copy-start(bf16[256,512]{1,0:T(8,128)(2,1)} %copy.52) | copy-start | bytes 786436
  76.6 20.3 %all-to-all-start.4 = ((bf16[16,32,512]{2,1,0:T(8,128)(2,1)}), bf16[16,32,512]{2,1,0:T(8,128)(2,1)}, u32[]{:S(2)}, u32[]{:S(2)}) async-start(bf16[16,32,512]{2,1,0:T(8,128)(2,1)} %bitcast.30), calls=%async_computation.4 | async-start | bytes 1048576 | tf_op jit(solution)/shard_map/all_to_all | solution.py:103
  96.9 20.2 %all-to-all-start.2 = ((bf16[16,32,512]{2,1,0:T(8,128)(2,1)}), bf16[16,32,512]{2,1,0:T(8,128)(2,1)S(1)}, u32[]{:S(2)}, u32[]{:S(2)}) async-start(bf16[16,32,512]{2,1,0:T(8,128)(2,1)} %bitcast.27), calls=%async_computation.2 | async-start | bytes 1048576 | tf_op jit(solution)/shard_map/all_to_all | solution.py:121
  100.4 90.9 %all-gather.3.cloned.1.call-start = ((), (), s32[]{:S(2)}) async-start(), calls=%async_computation.5 | async-start | bytes 1081344 | tf_op jit(solution)/shard_map/all_gather | solution.py:111
Sparse Core Ops, SparseCore 0:
  104.4 79.3 all-gather.2
where the time goes:
time: 226 us
  blocking collectives  116 us (51%)
  waiting for transfers between devices  43.2 us (19%)
  matrix products  20.1 us (9%)
  between operations  14.9 us (7%)
  starting transfers between devices  11.7 us (5%)
  other arithmetic  10.8 us (5%)
  local copies, waits for them, and re-layouts  8.98 us (4%)
    all_gather x1, blocking collectives, per_device(): lax.all_gather(summed, 'dp', axis=0, tiled=True).astype(jnp.float32)  40.4 us
    all_to_all x1, blocking collectives, per_device(): lax.all_to_all(local_grad.reshape(copies, part_rows, model_width), 'dp',...  31.6 us
    all_gather x1, blocking collectives, per_device(): lax.all_gather(dense_sum.astype(jnp.bfloat16), 'table', axis=0, tiled=True)  25.2 us
    all_to_all x1, blocking collectives, per_device(): lax.all_to_all(requested, 'table', split_axis=0, concat_axis=0, tiled=True)  18.6 us
    all_to_all x1, waiting for transfers between devices, per_device(): lax.all_to_all(reply.reshape(groups, capacity, model_width), 'table', spl...  16.6 us
    all_to_all x1, waiting for transfers between devices, per_device(): lax.all_to_all(outgoing.reshape(groups, capacity, model_width), 'table',...  14.9 us
    all_to_all x1, waiting for transfers between devices, per_device(): lax.all_to_all(dense_part.reshape(groups, dense_rows, model_width), 'tabl...  11.7 us
    dot_general x2, matrix products, hstu_layer(): jnp.dot(normed.reshape(samples_here * seq_span, model_width), w_in, prefe...  5.66 us
  transfers between devices with their start and end apart: 4, of which 3 were waited for; matrix products, arithmetic and copies ran while one was open for 4% of the time, Pallas kernels for 0%

commit v1 on v0

--- a/solution.py
+++ b/solution.py
@@ -110,7 +110,12 @@
     dense_block = jnp.sum(dense_terms.astype(jnp.float32), axis=0).astype(jnp.bfloat16)
     dense_blocks = lax.all_gather(dense_block, "dp", axis=0, tiled=False)
     dense_sum = jnp.sum(dense_blocks.astype(jnp.float32), axis=0) * grad_scale
-    dense_grad = lax.all_gather(dense_sum.astype(jnp.bfloat16), "table", axis=0, tiled=True)
+    dense_grad = jnp.concatenate(
+        lax.all_to_all(
+            jnp.stack([dense_sum.astype(jnp.bfloat16)] * lax.axis_size("table")), "table", 0, 0
+        ),
+        axis=0,
+    )
     (row_grad,) = pullback(flat_seed.astype(jnp.float32))
     outgoing = lax.dot_general(
         place,

time: 226 us -> 256 us (1.13)
  the two profiles are of different devices: /device:TPU:1 before, /device:TPU:64 now
where the time goes in v1:
time: 256 us; the launch traced here: 255 us
  waiting for transfers between devices  99.9 us (39%)
  blocking collectives  64.2 us (25%)
  starting transfers between devices  34.4 us (13%)
  matrix products  21 us (8%)
  between operations  14.9 us (6%)
  other arithmetic  10.8 us (4%)
  local copies, waits for them, and re-layouts  9.82 us (4%)
    all_gather x1, waiting for transfers between devices, per_device(): dense_blocks = lax.all_gather(dense_block, 'dp', axis=0, tiled=False)  63.6 us
    all_gather x1, blocking collectives, per_device(): lax.all_gather(summed, 'dp', axis=0, tiled=True).astype(jnp.float32)  48.3 us
    all_to_all x1, blocking collectives, per_device(): lax.all_to_all(requested, 'table', split_axis=0, concat_axis=0, tiled=True)  16 us
    all_to_all x1, waiting for transfers between devices, per_device(): lax.all_to_all(reply.reshape(groups, capacity, model_width), 'table', spl...  13.6 us
    all_to_all x1, waiting for transfers between devices, per_device(): lax.all_to_all(outgoing.reshape(groups, capacity, model_width), 'table',...  12.8 us
    all_to_all x1, starting transfers between devices, per_device(): lax.all_to_all(local_grad.reshape(copies, part_rows, model_width), 'dp',...  9.96 us
    all_to_all x1, waiting for transfers between devices, per_device(): lax.all_to_all(dense_part.reshape(groups, dense_rows, model_width), 'tabl...  9.9 us
    all_to_all x1, starting transfers between devices, per_device(): lax.all_to_all(jnp.stack([dense_sum.astype(jnp.bfloat16)] * lax.axis_size...  7.77 us
  transfers between devices with their start and end apart: 6, of which 4 were waited for; matrix products, arithmetic and copies ran while one was open for 4% of the time, Pallas kernels for 0%

profile of v1, /device:TPU:64, one launch (start us, length us, event | category | flops | bytes accessed | tf_op | source)
XLA Modules:
  0.0 255.1 jit_solution(9165055078764034867)
XLA Ops:
  11.2 16.0 %all_to_all.34 = s32[16,1,32]{2,1,0:T(1,128)S(1)} all-to-all(s32[16,1,32]{2,1,0:T(1,128)S(1)} %all_to_all.21), channel_id=1, replica_groups=mesh['dp'=32,'table'=16] {'table'}, dimensions={0} | all-to-all | bytes 4096 | tf_op jit(solution)/shard_map/all_to_all | solution.py:75
  28.4 2.5 fusion.17
  31.0 4.8 %all-to-all-start.1 = ((bf16[16,32,512]{2,1,0:T(8,128)(2,1)}), bf16[16,32,512]{2,1,0:T(8,128)(2,1)S(1)}, u32[]{:S(2)}, u32[]{:S(2)}) async-start(bf16[16,32,512]{2,1,0:T(8,128)(2,1)} %bitcast.6), calls=%async_computation.1 | async-start | bytes 1048576 | tf_op jit(solution)/shard_map/all_to_all | solution.py:81
  36.5 13.6 %all-to-all-done.1 = bf16[16,32,512]{2,1,0:T(8,128)(2,1)S(1)} async-done(((bf16[16,32,512]{2,1,0:T(8,128)(2,1)}), bf16[16,32,512]{2,1,0:T(8,128)(2,1)S(1)}, u32[]{:S(2)}, u32[]{:S(2)}) %all-to-all-start.1) | async-done | bytes 524320 | tf_op jit(solution)/shard_map/all_to_all | solution.py:81
  50.8 2.7 %fusion.70 = (bf16[256,2048]{1,0:T(8,128)(2,1)S(1)}, f32[256,2048]{1,0:T(8,128)}, f32[256,2048]{1,0:T(8,128)}) fusion(bf16[512,2048]{1,0:T(8,128)(2,1)S(1)} %copy-done, f32[256,512]{1,0:T(8,128)S(1)} %get-tuple-element.15, f32[256]{0:T(256)S(1)} %fusion.63, f32[256]{0:T(256)S(1)} %broadcast_multiply_fusion.1), kind=kOutput, calls=%fused_computation.113 | convolution fusion | flops 539885568 | bytes 7866368 | tf_op jit(solution)/shard_map/jvp()/dot_general | solution.py:22
  55.2 1.6 divide_convert_fusion
  59.2 1.8 multiply_reduce_fusion.1
  63.6 1.3 fusion.76
  64.9 2.0 fusion.31
  69.0 1.9 copy.50
  71.7 5.9 %all-to-all-start.4 = ((bf16[16,32,512]{2,1,0:T(8,128)(2,1)}), bf16[16,32,512]{2,1,0:T(8,128)(2,1)}, u32[]{:S(2)}, u32[]{:S(2)}) async-start(bf16[16,32,512]{2,1,0:T(8,128)(2,1)} %bitcast.30), calls=%async_computation.4 | async-start | bytes 1048576 | tf_op jit(solution)/shard_map/all_to_all | solution.py:103
  77.7 2.9 %multiply_reduce_fusion = (f32[256]{0:T(256)S(1)}, f32[256,512]{1,0:T(8,128)S(1)}) fusion(f32[256,512]{1,0:T(8,128)S(1)} %get-tuple-element.15, f32[256]{0:T(256)S(1)} %broadcast_multiply_fusion.1, bf16[512,2048]{1,0:T(8,128)(2,1)S(1)} %copy-done, f32[256,2048]{1,0:T(8,128)} %get-tuple-element.16, f32[256,512]{1,0:T(8,128)} %get-tuple-element.8, ...), kind=kOutput, calls=%fused_computation.56 | convolution fusion | flops 545390336 | bytes 6555648 | tf_op jit(solution)/shard_map/transpose(jvp())/dot_general | solution.py:22
  80.9 1.3 convolution_convert_fusion.2
  82.2 9.9 %all-to-all-done.4 = bf16[16,32,512]{2,1,0:T(8,128)(2,1)} async-done(((bf16[16,32,512]{2,1,0:T(8,128)(2,1)}), bf16[16,32,512]{2,1,0:T(8,128)(2,1)}, u32[]{:S(2)}, u32[]{:S(2)}) %all-to-all-start.4) | async-done | bytes 524320 | tf_op jit(solution)/shard_map/all_to_all | solution.py:103
  92.1 5.9 %all-to-all-start.2 = ((bf16[16,32,512]{2,1,0:T(8,128)(2,1)}), bf16[16,32,512]{2,1,0:T(8,128)(2,1)S(1)}, u32[]{:S(2)}, u32[]{:S(2)}) async-start(bf16[16,32,512]{2,1,0:T(8,128)(2,1)} %bitcast.27), calls=%async_computation.2 | async-start | bytes 1048576 | tf_op jit(solution)/shard_map/all_to_all | solution.py:126
  98.0 1.7 reduce_sum.150
  99.8 12.8 %all-to-all-done.2 = bf16[16,32,512]{2,1,0:T(8,128)(2,1)S(1)} async-done(((bf16[16,32,512]{2,1,0:T(8,128)(2,1)}), bf16[16,32,512]{2,1,0:T(8,128)(2,1)S(1)}, u32[]{:S(2)}, u32[]{:S(2)}) %all-to-all-start.2) | async-done | bytes 524320 | tf_op jit(solution)/shard_map/all_to_all | solution.py:126
  112.6 1.6 fusion.16
  114.1 10.0 %all-to-all-start.3 = ((bf16[32,24,512]{2,1,0:T(8,128)(2,1)}), bf16[32,24,512]{2,1,0:T(8,128)(2,1)S(1)}, u32[]{:S(2)}, u32[]{:S(2)}) async-start(bf16[32,24,512]{2,1,0:T(8,128)(2,1)} %bitcast.115), calls=%async_computation.3 | async-start | bytes 1572864 | tf_op jit(solution)/shard_map/all_to_all | solution.py:140
  124.1 63.6 %all-gather.3.cloned.1.call-done = bf16[1024,512]{1,0:T(8,128)(2,1)} async-done(((bf16[32,512]{1,0:T(8,128)(2,1)}), bf16[1024,512]{1,0:T(8,128)(2,1)}) %all-gather.3.cloned.1.call-update) | async-done | bytes 1048592 | tf_op jit(solution)/shard_map/all_gather | solution.py:111
  187.7 1.4 convert_reduce_fusion
  190.0 7.8 %all-to-all-start.5 = ((bf16[16,32,512]{2,1,0:T(8,128)(2,1)}), bf16[16,32,512]{2,1,0:T(8,128)(2,1)S(1)}, u32[]{:S(2)}, u32[]{:S(2)}) async-start(bf16[16,32,512]{2,1,0:T(8,128)(2,1)} %stack.2), calls=%async_computation.5 | async-start | bytes 1048576 | tf_op jit(solution)/shard_map/all_to_all | solution.py:114
  197.8 48.3 %all_gather.9 = bf16[768,512]{1,0:T(8,128)(2,1)S(1)} all-gather(bf16[24,512]{1,0:T(8,128)(2,1)S(1)} %reduce_sum.149), channel_id=1, replica_groups=mesh['dp'=32,'table'=16] {'dp'}, dimensions={0}, use_global_device_ids=true | all-gather | bytes 811008 | tf_op jit(solution)/shard_map/all_gather | solution.py:148
  246.1 1.4 convert_element_type.166
  (68 shorter events, 17.6 us)
Async XLA Ops:
  7.2 43.6 %copy-start = (bf16[512,2048]{1,0:T(8,128)(2,1)S(1)}, bf16[512,2048]{1,0:T(8,128)(2,1)}, u32[]{:S(2)}) copy-start(bf16[512,2048]{1,0:T(8,128)(2,1)} %param.11) | copy-start | bytes 6291460
  31.0 19.2 %all-to-all-start.1 = ((bf16[16,32,512]{2,1,0:T(8,128)(2,1)}), bf16[16,32,512]{2,1,0:T(8,128)(2,1)S(1)}, u32[]{:S(2)}, u32[]{:S(2)}) async-start(bf16[16,32,512]{2,1,0:T(8,128)(2,1)} %bitcast.6), calls=%async_computation.1 | async-start | bytes 1048576 | tf_op jit(solution)/shard_map/all_to_all | solution.py:81
  54.4 0.7 copy-start.5
  54.6 2.1 copy-start.7
  55.2 1.6 copy-start.9
  56.7 0.8 copy-start.3
  56.7 2.4 copy-start.2
  57.1 0.8 copy-start.1
  59.1 1.9 copy-start.4
  64.9 2.1 copy-start.6
  64.9 2.4 copy-start.8
  69.0 8.6 %copy-start.10 = (bf16[256,512]{1,0:T(8,128)(2,1)S(1)}, bf16[256,512]{1,0:T(8,128)(2,1)}, u32[]{:S(2)}) copy-start(bf16[256,512]{1,0:T(8,128)(2,1)} %copy.52) | copy-start | bytes 786436
  71.7 20.3 %all-to-all-start.4 = ((bf16[16,32,512]{2,1,0:T(8,128)(2,1)}), bf16[16,32,512]{2,1,0:T(8,128)(2,1)}, u32[]{:S(2)}, u32[]{:S(2)}) async-start(bf16[16,32,512]{2,1,0:T(8,128)(2,1)} %bitcast.30), calls=%async_computation.4 | async-start | bytes 1048576 | tf_op jit(solution)/shard_map/all_to_all | solution.py:103
  92.1 20.5 %all-to-all-start.2 = ((bf16[16,32,512]{2,1,0:T(8,128)(2,1)}), bf16[16,32,512]{2,1,0:T(8,128)(2,1)S(1)}, u32[]{:S(2)}, u32[]{:S(2)}) async-start(bf16[16,32,512]{2,1,0:T(8,128)(2,1)} %bitcast.27), calls=%async_computation.2 | async-start | bytes 1048576 | tf_op jit(solution)/shard_map/all_to_all | solution.py:126
  98.0 89.7 %all-gather.3.cloned.1.call-start = ((), (), s32[]{:S(2)}) async-start(), calls=%async_computation.6 | async-start | bytes 1081344 | tf_op jit(solution)/shard_map/all_gather | solution.py:111
  114.1 75.0 %all-to-all-start.3 = ((bf16[32,24,512]{2,1,0:T(8,128)(2,1)}), bf16[32,24,512]{2,1,0:T(8,128)(2,1)S(1)}, u32[]{:S(2)}, u32[]{:S(2)}) async-start(bf16[32,24,512]{2,1,0:T(8,128)(2,1)} %bitcast.115), calls=%async_computation.3 | async-start | bytes 1572864 | tf_op jit(solution)/shard_map/all_to_all | solution.py:140
  190.0 57.5 %all-to-all-start.5 = ((bf16[16,32,512]{2,1,0:T(8,128)(2,1)}), bf16[16,32,512]{2,1,0:T(8,128)(2,1)S(1)}, u32[]{:S(2)}, u32[]{:S(2)}) async-start(bf16[16,32,512]{2,1,0:T(8,128)(2,1)} %stack.2), calls=%async_computation.5 | async-start | bytes 1048576 | tf_op jit(solution)/shard_map/all_to_all | solution.py:114
Sparse Core Ops, SparseCore 0:
  102.0 85.6 all-gather.2
